TPU v7x, 256 devices: a whole 4x4x8 slice. The times are simulated.
256 devices in a mesh: dp: 16 (over z, core), mp: 16 (over y, x).
Axes of the slice: x: 4, y: 4, z: 8, core: 2. Of those that a mesh axis runs over, the one named last changes fastest.
Arguments:
- hidden_states: bfloat16 [256, 640, 1280], P(('dp', 'mp')), may hold values from -6 to 6
- ln_attn_gain: float32 [1280], replicated, may hold values from 0.1 to 1.9
- w_qkv: bfloat16 [1280, 16, 192], P(None, 'mp'), may hold values from -0.15625 to 0.15625
- output_weight: bfloat16 [64, 16, 1280], P(None, 'mp'), may hold values from -0.75 to 0.75
- ln_final_gain: float32 [1280], replicated, may hold values from 0.1 to 1.9
- dense_weight: bfloat16 [1280, 1280], replicated, may hold values from -0.15625 to 0.15625
- decoder_weight: bfloat16 [1280, 33], replicated, may hold values from -0.5390625 to 0.5390625
- decoder_bias: float32 [33], replicated, may hold values from -4 to 4
- seq_tokens: int32 [24, 640], replicated, may hold values from 4 to 23
- seq_lengths: int32 [24], replicated, may hold values from 128 to 640
- copy_sequence: int32 [256], replicated, may hold values from 0 to 23
- mask_code: int32 [256, 64], replicated, may hold values from 0 to 1048575
- copy_owner: int32 [256], replicated, may hold values from 0 to 255, each once
Outputs:
- pll: float32 [256, 64], P('dp', 'mp')
Inputs may be any that keep to these rules, and one draw needn't show every extreme that they name: `seq_tokens`: amino-acid token ids. `copy_owner`: every row of pll is named by exactly one copy.
All inputs are finite; a program needn't handle non-finite values.
Results may differ from a plain program's by a relative error of at most 0.0038.
Values may be sent and summed in bfloat16 or wider, within the bound.
No kernel may reach another device: no remote copies, remote signals or barrier semaphores. Data moves between devices by JAX's collectives and lax.ppermute only.
A program may use at most 128 MiB of HBM per device.

v0:
```python
import jax
import jax.numpy as jnp
from jax import lax
from jax.sharding import PartitionSpec as P

epsilon = 1e-05


def layer_norm(inputs):
    average = jnp.mean(inputs, axis=-1, keepdims=True)
    centred = inputs - average
    variance = jnp.mean(centred * centred, axis=-1, keepdims=True)
    return centred * lax.rsqrt(variance + epsilon)


def rotary_tables(seq_span, head_size):
    half_width = head_size // 2
    frequency = 1.0 / 10000.0 ** (jnp.arange(half_width, dtype=jnp.float32) * (2.0 / head_size))
    angles = jnp.arange(seq_span, dtype=jnp.float32)[:, None] * frequency[None, :]
    angles = jnp.concatenate([angles, angles], axis=-1)
    return (jnp.cos(angles), jnp.sin(angles))


def rotate(inputs, cosine, sine):
    half_width = inputs.shape[-1] // 2
    turned = jnp.concatenate([-inputs[..., half_width:], inputs[..., :half_width]], axis=-1)
    return inputs * cosine + turned * sine


def score_rows(residual, ln_final_gain, dense_weight, decoder_weight, decoder_bias, targets):
    feature = residual.shape[-1]
    normed_final = (layer_norm(residual) * ln_final_gain).astype(jnp.bfloat16).reshape(-1, feature)
    dense_out = jnp.dot(normed_final, dense_weight, preferred_element_type=jnp.float32)
    headed = layer_norm(jax.nn.gelu(dense_out, approximate=False)).astype(jnp.bfloat16)
    logits = jnp.dot(headed, decoder_weight, preferred_element_type=jnp.float32) + decoder_bias
    log_probs = logits - jax.nn.logsumexp(logits, axis=-1, keepdims=True)
    vocab_ids = jnp.arange(logits.shape[-1], dtype=jnp.int32)
    flat_targets = targets.reshape(-1)
    picked = jnp.sum(
        jnp.where(flat_targets[:, None] == vocab_ids[None, :], log_probs, 0.0), axis=-1
    )
    return picked.reshape(targets.shape)


def copy_meta(first, amount, tables):
    seq_tokens, seq_lengths, copy_sequence, mask_code = tables
    sequence = lax.dynamic_slice_in_dim(copy_sequence, first, amount, 0)
    codes = lax.dynamic_slice_in_dim(mask_code, first, amount, 0)
    seq_ids = jnp.arange(seq_lengths.shape[0], dtype=jnp.int32)
    lengths = jnp.sum(
        jnp.where(sequence[:, None] == seq_ids[None, :], seq_lengths[None, :], 0), axis=1
    )
    positions = codes % lengths[:, None]
    return (sequence, lengths, positions)


def attend_projected(projected, out_part, lengths, positions, cosine, sine):
    copies, seq_span, head_count, three, head_size = projected.shape
    key_matrix = rotate(
        projected[:, :, :, 1], cosine[None, :, None, :], sine[None, :, None, :]
    ).astype(jnp.bfloat16)
    value_matrix = projected[:, :, :, 2].astype(jnp.bfloat16)
    query_matrix = projected[jnp.arange(copies)[:, None], positions, :, 0] * head_size ** (-0.5)
    query_matrix = rotate(
        query_matrix, cosine[positions][:, :, None, :], sine[positions][:, :, None, :]
    ).astype(jnp.bfloat16)
    attention_logits = jnp.einsum(
        "cmhd,clhd->chml", query_matrix, key_matrix, preferred_element_type=jnp.float32
    )
    alive = jnp.arange(seq_span, dtype=jnp.int32)[None, :] < lengths[:, None]
    attention_logits = jnp.where(alive[:, None, None, :], attention_logits, -1e30)
    largest = jnp.max(attention_logits, axis=-1, keepdims=True)
    weights = jnp.exp(attention_logits - largest)
    attention_probs = (weights / jnp.sum(weights, axis=-1, keepdims=True)).astype(jnp.bfloat16)
    context_vectors = jnp.einsum(
        "chml,clhd->cmhd", attention_probs, value_matrix, preferred_element_type=jnp.float32
    ).astype(jnp.bfloat16)
    return jnp.einsum(
        "cmhd,dhe->cme", context_vectors, out_part, preferred_element_type=jnp.float32
    )


def on_device(
    hidden_states,
    ln_attn_gain,
    w_qkv,
    output_weight,
    ln_final_gain,
    dense_weight,
    decoder_weight,
    decoder_bias,
    seq_tokens,
    seq_lengths,
    copy_sequence,
    mask_code,
    copy_owner,
):
    lane_copies, seq_span, feature = hidden_states.shape
    model_size = lax.axis_size("mp")
    model_index = lax.axis_index("mp")
    group_copies = lane_copies * model_size
    head_size = output_weight.shape[0]
    mask_count = mask_code.shape[1]
    own_masks = mask_count // model_size
    cosine, sine = rotary_tables(seq_span, head_size)
    tables = (seq_tokens, seq_lengths, copy_sequence, mask_code)
    group_first = lax.axis_index("dp") * group_copies
    sequence, lengths, positions = copy_meta(group_first, group_copies, tables)
    targets = jnp.take_along_axis(seq_tokens[sequence], positions, axis=1)
    own_targets = lax.dynamic_slice_in_dim(targets, model_index * own_masks, own_masks, 1)
    lane_start = model_index * lane_copies
    lane_positions = lax.dynamic_slice_in_dim(positions, lane_start, lane_copies, 0)
    normed = (layer_norm(hidden_states.astype(jnp.float32)) * ln_attn_gain).astype(jnp.bfloat16)
    own_rows = hidden_states[jnp.arange(lane_copies)[:, None], lane_positions].astype(jnp.float32)
    lane_lengths = lax.dynamic_slice_in_dim(lengths, lane_start, lane_copies, 0)
    qkv_part = lax.all_gather(w_qkv, "mp", axis=1, tiled=True)
    out_part = lax.all_gather(output_weight, "mp", axis=1, tiled=True)
    count = qkv_part.shape[1]
    made = jnp.dot(
        normed.reshape(-1, feature),
        qkv_part.reshape(feature, -1),
        preferred_element_type=jnp.float32,
    )
    made = made.reshape(lane_copies, seq_span, count, 3, head_size)
    attention_mixed = attend_projected(made, out_part, lane_lengths, lane_positions, cosine, sine)
    lane_rows = own_rows + attention_mixed
    residual = lax.all_to_all(lane_rows, "mp", split_axis=1, concat_axis=0, tiled=True)
    attention_logits = score_rows(
        residual, ln_final_gain, dense_weight, decoder_weight, decoder_bias, own_targets
    )
    everything = lax.all_gather(attention_logits, "dp", axis=0, tiled=True)
    wanted = group_first + jnp.arange(group_copies, dtype=jnp.int32)
    copy_ids = jnp.arange(copy_owner.shape[0], dtype=jnp.int32)
    source = jnp.sum(
        jnp.where(copy_owner[None, :] == wanted[:, None], copy_ids[None, :], 0), axis=1
    )
    return everything[source]


def solution(mesh):
    placed = (
        P(("dp", "mp"), None, None),
        P(),
        P(None, "mp", None),
        P(None, "mp", None),
        P(),
        P(),
        P(),
        P(),
        P(),
        P(),
        P(),
        P(),
        P(),
    )
    return jax.shard_map(
        on_device, mesh=mesh, in_specs=placed, out_specs=P("dp", "mp"), check_vma=False
    )
```

profile of v0, /device:TPU:1, one launch (start us, length us, event | category | flops | bytes accessed | tf_op | source)
XLA Modules:
  0.0 194.8 jit_solution(9055554466586441534)
XLA Ops:
  6.5 0.7 all-gather.4.cloned.1.call-update
  8.0 0.8 compare_select_fusion.3
  8.8 0.8 select_reduce_fusion.3
  9.6 0.8 constant_dynamic-slice_fusion.1
  11.6 2.1 %fusion.52 = (f32[640,64]{1,0:T(8,128)}, f32[640,64]{1,0:T(8,128)}) fusion(f32[640,32]{1,0:T(8,128)S(1)} %iota_multiply_fusion), kind=kLoop, calls=%fused_computation.81 | loop fusion | flops 40960 | bytes 409600 | tf_op jit(solution)/shard_map/cos | solution.py:21
  13.7 1.2 iota_compare_fusion.2
  15.0 1.4 gather_fusion
  16.5 8.6 %gather_fusion.6 = s32[1024]{0:T(1024)S(1)} fusion(s32[16,640]{1,0:T(8,128)S(1)} %gather_fusion, s32[1024]{0:T(1024)S(1)} %reshape.339), kind=kCustom, calls=%fused_computation.6 | custom fusion | bytes 16384 | tf_op jit(solution)/shard_map/jit(take_along_axis)/gather | solution.py:109
  25.2 1.1 copy.41
  26.4 1.6 gather_fusion.3
  28.0 1.6 gather_fusion.4
  29.5 1.8 copy.42
  31.9 2.6 %gather_fusion.1 = bf16[64,1280]{1,0:T(8,128)(2,1)} fusion(bf16[1,640,1280]{2,1,0:T(8,128)(2,1)} %param.13, s32[64]{0:T(128)S(1)} %or_bitcast_fusion.1), kind=kCustom, calls=%fused_computation.1 | custom fusion | bytes 328192 | tf_op jit(solution)/shard_map/gather | solution.py:114
  35.2 1.8 convert_reduce_fusion
  37.5 49.6 %all-gather.4.cloned.1.call-done = bf16[1280,16,192]{0,2,1:T(8,128)(2,1)} async-done(((bf16[1280,1,192]{0,2,1:T(8,128)(2,1)}), bf16[1280,16,192]{0,2,1:T(8,128)(2,1)}) %all-gather.4.cloned.1.call-update) | async-done | bytes 7864336 | tf_op jit(solution)/shard_map/all_gather | solution.py:116
  87.2 11.3 %convolution_bitcast_fusion = f32[1,640,16,3,64]{1,4,3,2,0:T(8,128)} fusion(bf16[16,3,64,1280]{3,2,1,0:T(8,128)(2,1)} %bitcast.96, bf16[1,640,1280]{2,1,0:T(8,128)(2,1)} %param.13, f32[1280]{0:T(1024)} %param.14, f32[640]{0:T(1024)S(1)} %add_rsqrt_fusion, f32[640]{0:T(1024)S(1)} %broadcast_multiply_fusion.1), kind=kOutput, calls=%fused_computation.15 | convolution fusion | flops 5037260800 | bytes 17377280 | tf_op jit(solution)/shard_map/dot_general | solution.py:119
  98.5 15.1 %copy.40 = f32[1,640,16,3,64]{4,2,3,1,0:T(8,128)} copy(f32[1,640,16,3,64]{1,4,3,2,0:T(8,128)} %convolution_bitcast_fusion) | data formatting | bytes 15728640 | tf_op jit(solution)/shard_map/dot_general | solution.py:119
  113.6 7.0 %gather_fusion.2 = f32[64,16,64]{2,1,0:T(8,128)} fusion(f32[1,640,16,3,64]{4,2,3,1,0:T(8,128)} %copy.40, s32[64]{0:T(128)S(1)} %or_bitcast_fusion), kind=kCustom, calls=%fused_computation.2 | custom fusion | bytes 525056 | tf_op jit(solution)/shard_map/gather | solution.py:63
  120.6 1.1 multiply_bitcast_fusion
  122.2 1.9 slice_bitcast_fusion
  124.3 0.7 copy-done.3
  125.0 2.6 %fusion.18 = f32[16,64,640]{2,1,0:T(8,128)S(1)} fusion(f32[640,16,32]{0,2,1:T(8,128)S(1)} %get-tuple-element.10, f32[640,16,32]{0,2,1:T(8,128)S(1)} %get-tuple-element.9, f32[1,640,16,3,64]{1,4,3,2,0:T(8,128)} %convolution_bitcast_fusion, f32[640,64]{0,1:T(8,128)S(1)} %copy-done.3, f32[640,64]{0,1:T(8,128)S(1)} %copy.41, bf16[64,16,64]{2,1,0:T(8,128)(2,1)S(1)} %fusion.38), kind=kOutput, calls=%fused_computation.33 | convolution fusion | flops 87162880 | bytes 8323072 | tf_op jit(solution)/shard_map/cmhd,clhd->chml/dot_general | solution.py:67
  127.7 2.1 %fusion.66 = (f32[16,64]{1,0:T(8,128)S(1)}, f32[16,64,640]{2,1,0:T(8,128)}) fusion(f32[16,64,640]{2,1,0:T(8,128)S(1)} %fusion.18, pred[640]{0:T(1024)(128)(4,1)S(1)} %copy-done.8), kind=kOutput, calls=%fused_computation.128 | output fusion | flops 2622079 | bytes 5247616 | tf_op jit(solution)/shard_map/sub | solution.py:73
  129.8 10.5 %all-gather.6.cloned.1.call-done = bf16[64,16,1280]{2,0,1:T(8,128)(2,1)} async-done(((bf16[64,1,1280]{2,0,1:T(8,128)(2,1)}), bf16[64,16,1280]{2,0,1:T(8,128)(2,1)}) %all-gather.6.cloned.1.call-update) | async-done | bytes 2621456 | tf_op jit(solution)/shard_map/all_gather | solution.py:117
  140.3 5.1 %fusion.9 = f32[1,64,1280]{2,1,0:T(8,128)} fusion(bf16[64,16,1280]{2,0,1:T(8,128)(2,1)} %all-gather.6.cloned.1.call-done, f32[16,64,640]{2,1,0:T(8,128)} %get-tuple-element.16, f32[16,64]{1,0:T(8,128)S(1)} %get-tuple-element.15, f32[1,640,16,3,64]{1,4,3,2,0:T(8,128)} %convolution_bitcast_fusion, bf16[64,1280]{1,0:T(8,128)(2,1)S(1)} %copy-done.4), kind=kOutput, calls=%fused_computation.26 | convolution fusion | flops 253198336 | bytes 7049216 | tf_op jit(solution)/shard_map/cmhd,dhe->cme/dot_general | solution.py:78
  145.5 2.0 %copy.45 = f32[1,64,1280]{2,0,1:T(1,128)} copy(f32[1,64,1280]{2,1,0:T(8,128)} %fusion.9) | data formatting | bytes 655360 | tf_op jit(solution)/shard_map/add | solution.py:126
  147.5 4.4 %all-to-all-start = ((f32[1,64,1280]{2,0,1:T(1,128)}), f32[1,64,1280]{2,0,1:T(1,128)}, u32[]{:S(2)}, u32[]{:S(2)}) async-start(f32[1,64,1280]{2,0,1:T(1,128)} %copy.45), calls=%async_computation | async-start | bytes 655360 | tf_op jit(solution)/shard_map/all_to_all | solution.py:127
  151.9 7.8 %all-to-all-done = f32[1,64,1280]{2,0,1:T(1,128)} async-done(((f32[1,64,1280]{2,0,1:T(1,128)}), f32[1,64,1280]{2,0,1:T(1,128)}, u32[]{:S(2)}, u32[]{:S(2)}) %all-to-all-start) | async-done | bytes 327712 | tf_op jit(solution)/shard_map/all_to_all | solution.py:127
  159.7 1.5 reduce_sum.105
  161.3 2.0 %multiply_reduce_fusion.1 = f32[64]{0:T(128)S(1)} fusion(f32[1,64,1280]{2,0,1:T(1,128)} %all-to-all-done, f32[64]{0:T(128)S(1)} %broadcast_multiply_fusion.3), kind=kLoop, calls=%fused_computation.76 | loop fusion | flops 245696 | bytes 328192 | tf_op jit(solution)/shard_map/reduce_sum | solution.py:12
  163.3 2.3 %fusion.67 = (f32[64]{0:T(128)S(1)}, f32[64,1280]{1,0:T(8,128)S(1)}) fusion(bf16[1280,1280]{1,0:T(8,128)(2,1)S(1)} %copy-done, f32[1,64,1280]{2,0,1:T(1,128)} %all-to-all-done, f32[1280]{0:T(1024)S(1)} %copy-done.11, f32[64]{0:T(128)S(1)} %add_rsqrt_fusion.2, f32[64]{0:T(128)S(1)} %broadcast_multiply_fusion.3), kind=kOutput, calls=%fused_computation.129 | convolution fusion | flops 215367616 | bytes 3938048 | tf_op jit(solution)/shard_map/dot_general | solution.py:33
  166.4 20.2 %all-gather = f32[16,16,4]{1,2,0:T(4,128)S(1)} all-gather(f32[1,16,4]{1,2,0:T(4,128)S(1)} %copy.46), channel_id=1, replica_groups=mesh['dp'=16,'mp'=16] {'dp'}, dimensions={0}, use_global_device_ids=true | all-gather | bytes 4352 | tf_op jit(solution)/shard_map/all_gather | solution.py:131
  (73 shorter events, 6.7 us)
Async XLA Ops:
  6.5 156.7 %copy-start = (bf16[1280,1280]{1,0:T(8,128)(2,1)S(1)}, bf16[1280,1280]{1,0:T(8,128)(2,1)}, u32[]{:S(2)}) copy-start(bf16[1280,1280]{1,0:T(8,128)(2,1)} %param.18) | copy-start | bytes 9830404
  6.5 80.7 %all-gather.4.cloned.1.call-start = ((), (), s32[]{:S(2)}) async-start(), calls=%async_computation.1 | async-start | bytes 8355840 | tf_op jit(solution)/shard_map/all_gather | solution.py:116
  7.3 133.1 %all-gather.6.cloned.1.call-start = ((), (), s32[]{:S(2)}) async-start(), calls=%async_computation.2 | async-start | bytes 2785280 | tf_op jit(solution)/shard_map/all_gather | solution.py:117
  25.1 9.4 %copy-start.7 = (s32[256]{0:T(256)S(1)}, s32[256]{0:T(256)}, u32[]{:S(2)}) copy-start(s32[256]{0:T(256)} %param.25) | copy-start | bytes 3076
  34.5 2.5 %copy-start.1 = (bf16[1,640,1280]{2,1,0:T(8,128)(2,1)S(1)}, bf16[1,640,1280]{2,1,0:T(8,128)(2,1)}, u32[]{:S(2)}) copy-start(bf16[1,640,1280]{2,1,0:T(8,128)(2,1)} %param.13) | copy-start | bytes 4915204
  120.6 1.4 copy-start.2
  124.1 0.9 copy-start.3
  125.0 2.6 %copy-start.8 = (pred[640]{0:T(1024)(128)(4,1)S(1)}, pred[640]{0:T(1024)(128)(4,1)}, u32[]{:S(2)}) copy-start(pred[640]{0:T(1024)(128)(4,1)} %iota_compare_fusion.2) | copy-start | bytes 1924
  127.7 12.7 %copy-start.4 = (bf16[64,1280]{1,0:T(8,128)(2,1)S(1)}, bf16[64,1280]{1,0:T(8,128)(2,1)}, u32[]{:S(2)}) copy-start(bf16[64,1280]{1,0:T(8,128)(2,1)} %gather_fusion.1) | copy-start | bytes 491524
  140.3 11.6 %copy-start.10 = (s32[16]{0:T(128)S(1)}, s32[16]{0:T(128)}, u32[]{:S(2)}) copy-start(s32[16]{0:T(128)} %select_reduce_fusion.2) | copy-start | bytes 196
  140.3 22.9 %copy-start.11 = (f32[1280]{0:T(1024)S(1)}, f32[1280]{0:T(1024)}, u32[]{:S(2)}) copy-start(f32[1280]{0:T(1024)} %param.17) | copy-start | bytes 15364
  147.5 12.2 %all-to-all-start = ((f32[1,64,1280]{2,0,1:T(1,128)}), f32[1,64,1280]{2,0,1:T(1,128)}, u32[]{:S(2)}, u32[]{:S(2)}) async-start(f32[1,64,1280]{2,0,1:T(1,128)} %copy.45), calls=%async_computation | async-start | bytes 655360 | tf_op jit(solution)/shard_map/all_to_all | solution.py:127
  163.3 2.6 %copy-start.5 = (bf16[1280,33]{0,1:T(8,128)(2,1)S(1)}, bf16[1280,33]{0,1:T(8,128)(2,1)}, u32[]{:S(2)}) copy-start(bf16[1280,33]{0,1:T(8,128)(2,1)} %param.19) | copy-start | bytes 253444
  163.3 2.6 %copy-start.9 = (f32[33]{0:T(128)S(1)}, f32[33]{0:T(128)}, u32[]{:S(2)}) copy-start(f32[33]{0:T(128)} %param.20) | copy-start | bytes 400
  163.3 2.9 %copy-start.6 = (s32[64]{0:T(128)S(1)}, s32[64]{0:T(128)}, u32[]{:S(2)}) copy-start(s32[64]{0:T(128)} %eq.57) | copy-start | bytes 772
Sparse Core Ops, SparseCore 0:
  9.8 77.3 all-gather.3
  89.6 50.6 all-gather.5
where the time goes:
time: 196 us; the launch traced here: 195 us
  waiting for transfers between devices  69.4 us (35%)
  local copies, waits for them, and re-layouts  49.3 us (25%)
  matrix products  21.6 us (11%)
  blocking collectives  20.2 us (10%)
  other arithmetic  16.1 us (8%)
  between operations  13.7 us (7%)
  starting transfers between devices  4.43 us (2%)
    all_gather x1, waiting for transfers between devices, on_device(): qkv_part = lax.all_gather(w_qkv, 'mp', axis=1, tiled=True)  49.6 us
    all_gather x1, blocking collectives, on_device(): everything = lax.all_gather(attention_logits, 'dp', axis=0, tiled=True)  20.2 us
    dot_general x1, local copies, waits for them, and re-layouts, on_device(): jnp.dot(normed.reshape(-1, feature), qkv_part.reshape(feature, -1), prefe...  15.1 us
    dot_general x1, matrix products, on_device(): jnp.dot(normed.reshape(-1, feature), qkv_part.reshape(feature, -1), prefe...  11.3 us
    all_gather x1, waiting for transfers between devices, on_device(): out_part = lax.all_gather(output_weight, 'mp', axis=1, tiled=True)  10.5 us
    gather x4, local copies, waits for them, and re-layouts, on_device(): targets = jnp.take_along_axis(seq_tokens[sequence], positions, axis=1)  10.2 us
    all_to_all x1, waiting for transfers between devices, on_device(): lax.all_to_all(lane_rows, 'mp', split_axis=1, concat_axis=0, tiled=True)  7.8 us
    gather x1, local copies, waits for them, and re-layouts, attend_projected(): projected[jnp.arange(copies)[:, None], positions, :, 0]  6.96 us
  transfers between devices with their start and end apart: 3, of which 3 were waited for; matrix products, arithmetic and copies ran while one was open for 37% of the time, Pallas kernels for 0%

commit v1 on v0

--- a/solution.py
+++ b/solution.py
@@ -114,7 +114,12 @@
     own_rows = hidden_states[jnp.arange(lane_copies)[:, None], lane_positions].astype(jnp.float32)
     lane_lengths = lax.dynamic_slice_in_dim(lengths, lane_start, lane_copies, 0)
     qkv_part = lax.all_gather(w_qkv, "mp", axis=1, tiled=True)
-    out_part = lax.all_gather(output_weight, "mp", axis=1, tiled=True)
+    ring = [output_weight]
+    for hop in range(15):
+        ring.append(lax.ppermute(ring[-1], "mp", [(dev, (dev + 1) % 16) for dev in range(16)]))
+    out_part = jnp.roll(
+        jnp.concatenate(ring[::-1], axis=1), (lax.axis_index("mp") + 1) * ring[0].shape[1], axis=1
+    )
     count = qkv_part.shape[1]
     made = jnp.dot(
         normed.reshape(-1, feature),

time: 196 us -> 319 us (1.63)
  local copies, waits for them, and re-layouts: 49.3 us -> 96.5 us
  waiting for transfers between devices: 69.4 us -> 112 us
  blocking collectives: 20.2 us -> 38.7 us
  other arithmetic: 16.1 us -> 24.4 us
  starting transfers between devices: 4.43 us -> 9.56 us
    ppermute x0 -> x15, waiting for transfers between devices: none -> 104 us  [on_device(): lax.ppermute(ring[-1], 'mp', [(dev, (dev + 1) % 16) for dev in range(16)])]
    all_gather x1, waiting for transfers between devices: 49.6 us -> 0.01 us  [on_device(): qkv_part = lax.all_gather(w_qkv, 'mp', axis=1, tiled=True)]
    unnamed x27 -> x106, local copies, waits for them, and re-layouts: 0.98 us -> 40.7 us
    all_gather x1, blocking collectives: 20.2 us -> 38.7 us  [on_device(): everything = lax.all_gather(attention_logits, 'dp', axis=0, tiled=True)]
    all_gather x1 -> x0, waiting for transfers between devices: 10.5 us -> none  [on_device(): out_part = lax.all_gather(output_weight, 'mp', axis=1, tiled=True)]
    gather x4, local copies, waits for them, and re-layouts: 10.2 us -> 14.6 us  [on_device(): targets = jnp.take_along_axis(seq_tokens[sequence], positions, axis=1)]
  transfers between devices with their start and end apart: 3 -> 17, of which waited for: 3 -> 14; matrix products, arithmetic and copies ran while one was open for 37% -> 26% of each run, Pallas kernels for 0% -> 0%
where the time goes in v1:
time: 319 us; the launch traced here: 317 us
  waiting for transfers between devices  112 us (35%)
  local copies, waits for them, and re-layouts  96.5 us (30%)
  blocking collectives  38.7 us (12%)
  other arithmetic  24.4 us (8%)
  matrix products  21.7 us (7%)
  between operations  13.9 us (4%)
  starting transfers between devices  9.56 us (3%)
    ppermute x15, waiting for transfers between devices, on_device(): lax.ppermute(ring[-1], 'mp', [(dev, (dev + 1) % 16) for dev in range(16)])  104 us
    unnamed x106, local copies, waits for them, and re-layouts  40.7 us
    all_gather x1, blocking collectives, on_device(): everything = lax.all_gather(attention_logits, 'dp', axis=0, tiled=True)  38.7 us
    dot_general x1, local copies, waits for them, and re-layouts, on_device(): jnp.dot(normed.reshape(-1, feature), qkv_part.reshape(feature, -1), prefe...  15.1 us
    gather x4, local copies, waits for them, and re-layouts, on_device(): targets = jnp.take_along_axis(seq_tokens[sequence], positions, axis=1)  14.6 us
    dot_general x1, matrix products, on_device(): jnp.dot(normed.reshape(-1, feature), qkv_part.reshape(feature, -1), prefe...  11.3 us
    all_to_all x1, waiting for transfers between devices, on_device(): lax.all_to_all(lane_rows, 'mp', split_axis=1, concat_axis=0, tiled=True)  7.92 us
    all_to_all x1, starting transfers between devices, on_device(): lax.all_to_all(lane_rows, 'mp', split_axis=1, concat_axis=0, tiled=True)  7.35 us
  transfers between devices with their start and end apart: 17, of which 14 were waited for; matrix products, arithmetic and copies ran while one was open for 26% of the time, Pallas kernels for 0%

profile of v1, /device:TPU:1, one launch (start us, length us, event | category | flops | bytes accessed | tf_op | source)
XLA Modules:
  0.0 316.9 jit_solution(18427871409411553021)
XLA Ops:
  7.3 2.1 collective-permute-start
  12.8 3.3 %collective-permute-done = bf16[64,1,1280]{2,0,1:T(8,128)(2,1)S(1)} collective-permute-done((bf16[64,1,1280]{2,0,1:T(8,128)(2,1)}, bf16[64,1,1280]{2,0,1:T(8,128)(2,1)S(1)}, u32[]{:S(2)}, u32[]{:S(2)}) %collective-permute-start) | collective-permute-done | bytes 163872 | tf_op jit(solution)/shard_map/ppermute | solution.py:119
  16.0 7.6 %collective-permute-done.1 = bf16[64,1,1280]{2,0,1:T(8,128)(2,1)} collective-permute-done((bf16[64,1,1280]{2,0,1:T(8,128)(2,1)S(1)}, bf16[64,1,1280]{2,0,1:T(8,128)(2,1)}, u32[]{:S(2)}, u32[]{:S(2)}) %collective-permute-start.1) | collective-permute-done | bytes 163872 | tf_op jit(solution)/shard_map/ppermute | solution.py:119
  24.4 7.1 %collective-permute-done.2 = bf16[64,1,1280]{2,0,1:T(8,128)(2,1)} collective-permute-done((bf16[64,1,1280]{2,0,1:T(8,128)(2,1)}, bf16[64,1,1280]{2,0,1:T(8,128)(2,1)}, u32[]{:S(2)}, u32[]{:S(2)}) %collective-permute-start.2) | collective-permute-done | bytes 163872 | tf_op jit(solution)/shard_map/ppermute | solution.py:119
  32.1 3.1 fusion.61
  36.8 6.6 %collective-permute-done.3 = bf16[64,1,1280]{2,0,1:T(8,128)(2,1)} collective-permute-done((bf16[64,1,1280]{2,0,1:T(8,128)(2,1)}, bf16[64,1,1280]{2,0,1:T(8,128)(2,1)}, u32[]{:S(2)}, u32[]{:S(2)}) %collective-permute-start.3) | collective-permute-done | bytes 163872 | tf_op jit(solution)/shard_map/ppermute | solution.py:119
  45.0 6.0 %collective-permute-done.4 = bf16[64,1,1280]{2,0,1:T(8,128)(2,1)S(1)} collective-permute-done((bf16[64,1,1280]{2,0,1:T(8,128)(2,1)}, bf16[64,1,1280]{2,0,1:T(8,128)(2,1)S(1)}, u32[]{:S(2)}, u32[]{:S(2)}) %collective-permute-start.4) | collective-permute-done | bytes 163872 | tf_op jit(solution)/shard_map/ppermute | solution.py:119
  51.0 9.9 %collective-permute-done.5 = bf16[64,1,1280]{2,0,1:T(8,128)(2,1)S(1)} collective-permute-done((bf16[64,1,1280]{2,0,1:T(8,128)(2,1)S(1)}, bf16[64,1,1280]{2,0,1:T(8,128)(2,1)S(1)}, u32[]{:S(2)}, u32[]{:S(2)}) %collective-permute-start.5) | collective-permute-done | bytes 163872 | tf_op jit(solution)/shard_map/ppermute | solution.py:119
  61.0 2.0 fusion.3
  63.0 10.4 %collective-permute-done.6 = bf16[64,1,1280]{2,0,1:T(8,128)(2,1)S(1)} collective-permute-done((bf16[64,1,1280]{2,0,1:T(8,128)(2,1)S(1)}, bf16[64,1,1280]{2,0,1:T(8,128)(2,1)S(1)}, u32[]{:S(2)}, u32[]{:S(2)}) %collective-permute-start.6) | collective-permute-done | bytes 163872 | tf_op jit(solution)/shard_map/ppermute | solution.py:119
  74.1 12.2 %collective-permute-done.7 = bf16[64,1,1280]{2,0,1:T(8,128)(2,1)S(1)} collective-permute-done((bf16[64,1,1280]{2,0,1:T(8,128)(2,1)S(1)}, bf16[64,1,1280]{2,0,1:T(8,128)(2,1)S(1)}, u32[]{:S(2)}, u32[]{:S(2)}) %collective-permute-start.7) | collective-permute-done | bytes 163872 | tf_op jit(solution)/shard_map/ppermute | solution.py:119
  86.3 12.6 %collective-permute-done.8 = bf16[64,1,1280]{2,0,1:T(8,128)(2,1)S(1)} collective-permute-done((bf16[64,1,1280]{2,0,1:T(8,128)(2,1)S(1)}, bf16[64,1,1280]{2,0,1:T(8,128)(2,1)S(1)}, u32[]{:S(2)}, u32[]{:S(2)}) %collective-permute-start.8) | collective-permute-done | bytes 163872 | tf_op jit(solution)/shard_map/ppermute | solution.py:119
  99.5 6.9 %collective-permute-done.9 = bf16[64,1,1280]{2,0,1:T(8,128)(2,1)S(1)} collective-permute-done((bf16[64,1,1280]{2,0,1:T(8,128)(2,1)S(1)}, bf16[64,1,1280]{2,0,1:T(8,128)(2,1)S(1)}, u32[]{:S(2)}, u32[]{:S(2)}) %collective-permute-start.9) | collective-permute-done | bytes 163872 | tf_op jit(solution)/shard_map/ppermute | solution.py:119
  106.4 7.4 %collective-permute-done.10 = bf16[64,1,1280]{2,0,1:T(8,128)(2,1)S(1)} collective-permute-done((bf16[64,1,1280]{2,0,1:T(8,128)(2,1)S(1)}, bf16[64,1,1280]{2,0,1:T(8,128)(2,1)S(1)}, u32[]{:S(2)}, u32[]{:S(2)}) %collective-permute-start.10) | collective-permute-done | bytes 163872 | tf_op jit(solution)/shard_map/ppermute | solution.py:119
  115.2 6.2 %collective-permute-done.11 = bf16[64,1,1280]{2,0,1:T(8,128)(2,1)S(1)} collective-permute-done((bf16[64,1,1280]{2,0,1:T(8,128)(2,1)S(1)}, bf16[64,1,1280]{2,0,1:T(8,128)(2,1)S(1)}, u32[]{:S(2)}, u32[]{:S(2)}) %collective-permute-start.11) | collective-permute-done | bytes 163872 | tf_op jit(solution)/shard_map/ppermute | solution.py:119
  121.4 7.6 %collective-permute-done.12 = bf16[64,1,1280]{2,0,1:T(8,128)(2,1)} collective-permute-done((bf16[64,1,1280]{2,0,1:T(8,128)(2,1)S(1)}, bf16[64,1,1280]{2,0,1:T(8,128)(2,1)}, u32[]{:S(2)}, u32[]{:S(2)}) %collective-permute-start.12) | collective-permute-done | bytes 163872 | tf_op jit(solution)/shard_map/ppermute | solution.py:119
  131.0 13.0 %gather_fusion.6 = s32[1024]{0:T(1024)} fusion(s32[16,640]{1,0:T(8,128)S(1)} %gather_fusion, s32[1024]{0:T(1024)S(1)} %reshape.339), kind=kCustom, calls=%fused_computation.6 | custom fusion | bytes 16384 | tf_op jit(solution)/shard_map/jit(take_along_axis)/gather | solution.py:109
  150.9 2.5 gather_fusion.1
  195.6 11.3 %convolution_bitcast_fusion = f32[1,640,16,3,64]{1,4,3,2,0:T(8,128)} fusion(bf16[16,3,64,1280]{3,2,1,0:T(8,128)(2,1)} %bitcast.95, bf16[1,640,1280]{2,1,0:T(8,128)(2,1)} %param.13, f32[1280]{0:T(1024)S(1)} %copy-done.33, f32[640]{0:T(1024)S(1)} %copy-done.30, f32[640]{0:T(1024)S(1)} %copy-done.28), kind=kOutput, calls=%fused_computation.15 | convolution fusion | flops 5037260800 | bytes 17377280 | tf_op jit(solution)/shard_map/dot_general | solution.py:124
  206.9 15.1 %copy.40 = f32[1,640,16,3,64]{4,2,3,1,0:T(8,128)} copy(f32[1,640,16,3,64]{1,4,3,2,0:T(8,128)} %convolution_bitcast_fusion) | data formatting | bytes 15728640 | tf_op jit(solution)/shard_map/dot_general | solution.py:124
  222.0 3.5 %slice_bitcast_fusion = f32[1,640,16,64]{1,3,2,0:T(8,128)} fusion(f32[1,640,16,3,64]{1,4,3,2,0:T(8,128)} %convolution_bitcast_fusion), kind=kLoop, calls=%fused_computation.25 | loop fusion | bytes 5242880 | tf_op jit(solution)/shard_map/squeeze | solution.py:60
  225.6 7.0 %gather_fusion.2 = f32[64,16,64]{2,1,0:T(8,128)} fusion(f32[1,640,16,3,64]{4,2,3,1,0:T(8,128)} %copy.40, s32[64]{0:T(128)S(1)} %or_bitcast_fusion), kind=kCustom, calls=%fused_computation.2 | custom fusion | bytes 525056 | tf_op jit(solution)/shard_map/gather | solution.py:63
  233.9 1.9 fusion.32
  236.1 2.6 fusion.27
  238.7 2.1 fusion.76
  240.9 5.2 %fusion.16 = f32[1,64,1280]{2,1,0:T(8,128)} fusion(bf16[64,32,1280]{2,0,1:T(8,128)(2,1)} %constant_dynamic-update-slice_fusion, s32[]{:T(128)S(6)} %select_n.108, f32[16,64,640]{2,1,0:T(8,128)} %get-tuple-element.16, f32[16,64]{1,0:T(8,128)S(1)} %get-tuple-element.15, f32[1,640,16,3,64]{1,4,3,2,0:T(8,128)} %convolution_bitcast_fusion, ...), kind=kOutput, calls=%fused_computation.28 | convolution fusion | flops 253198336 | bytes 7049220 | tf_op jit(solution)/shard_map/cmhd,dhe->cme/dot_general | solution.py:78
  246.0 2.0 copy.45
  248.1 7.4 %all-to-all-start = ((f32[1,64,1280]{2,0,1:T(1,128)}), f32[1,64,1280]{2,0,1:T(1,128)}, u32[]{:S(2)}, u32[]{:S(2)}) async-start(f32[1,64,1280]{2,0,1:T(1,128)} %copy.45), calls=%async_computation | async-start | bytes 655360 | tf_op jit(solution)/shard_map/all_to_all | solution.py:132
  255.5 7.9 %all-to-all-done = f32[1,64,1280]{2,0,1:T(1,128)} async-done(((f32[1,64,1280]{2,0,1:T(1,128)}), f32[1,64,1280]{2,0,1:T(1,128)}, u32[]{:S(2)}, u32[]{:S(2)}) %all-to-all-start) | async-done | bytes 327712 | tf_op jit(solution)/shard_map/all_to_all | solution.py:132
  264.9 2.0 multiply_reduce_fusion.1
  266.9 2.3 fusion.77
  270.0 38.7 %all-gather = f32[16,16,4]{1,2,0:T(4,128)S(1)} all-gather(f32[1,16,4]{1,2,0:T(4,128)S(1)} %copy.46), channel_id=1, replica_groups=mesh['dp'=16,'mp'=16] {'dp'}, dimensions={0}, use_global_device_ids=true | all-gather | bytes 4352 | tf_op jit(solution)/shard_map/all_gather | solution.py:136
  (179 shorter events, 67.7 us)
Async XLA Ops:
  6.5 260.4 %copy-start = (bf16[1280,1280]{1,0:T(8,128)(2,1)S(1)}, bf16[1280,1280]{1,0:T(8,128)(2,1)}, u32[]{:S(2)}) copy-start(bf16[1280,1280]{1,0:T(8,128)(2,1)} %param.18) | copy-start | bytes 9830404
  6.5 123.7 %copy-start.2 = (s32[24,640]{1,0:T(8,128)S(1)}, s32[24,640]{1,0:T(8,128)}, u32[]{:S(2)}) copy-start(s32[24,640]{1,0:T(8,128)} %param.21) | copy-start | bytes 184324
  6.5 189.1 %all-gather.3.cloned.1.call-start = ((), (), s32[]{:S(2)}) async-start(), calls=%async_computation.1 | async-start | bytes 8355840 | tf_op jit(solution)/shard_map/all_gather | solution.py:116
  7.3 8.8 %collective-permute-start = (bf16[64,1,1280]{2,0,1:T(8,128)(2,1)}, bf16[64,1,1280]{2,0,1:T(8,128)(2,1)S(1)}, u32[]{:S(2)}, u32[]{:S(2)}) collective-permute-start(bf16[64,1,1280]{2,0,1:T(8,128)(2,1)} %param.16), channel_id=1, source_target_pairs={{0,1},{1,2},{2,3},{3,4},{4,5},{5,6},{6,7},{7,8},{8,9},{9,10},{10,1... | collective-permute-start | bytes 491528 | tf_op jit(solution)/shard_map/ppermute | solution.py:119
  16.0 114.9 %copy-start.4 = (bf16[64,1,1280]{2,0,1:T(8,128)(2,1)}, bf16[64,1,1280]{2,0,1:T(8,128)(2,1)S(1)}, u32[]{:S(2)}) copy-start(bf16[64,1,1280]{2,0,1:T(8,128)(2,1)S(1)} %collective-permute-done) | copy-start | bytes 491524
  16.0 7.6 %collective-permute-start.1 = (bf16[64,1,1280]{2,0,1:T(8,128)(2,1)S(1)}, bf16[64,1,1280]{2,0,1:T(8,128)(2,1)}, u32[]{:S(2)}, u32[]{:S(2)}) collective-permute-start(bf16[64,1,1280]{2,0,1:T(8,128)(2,1)S(1)} %collective-permute-done), channel_id=1, source_target_pairs={{0,1},{1,2},{2,3},{3,4},{4,5},{5,6},{6,7},{7,8},{8,9},{9,10},{10,1... | collective-permute-start | bytes 491528 | tf_op jit(solution)/shard_map/ppermute | solution.py:119
  23.6 7.9 %collective-permute-start.2 = (bf16[64,1,1280]{2,0,1:T(8,128)(2,1)}, bf16[64,1,1280]{2,0,1:T(8,128)(2,1)}, u32[]{:S(2)}, u32[]{:S(2)}) collective-permute-start(bf16[64,1,1280]{2,0,1:T(8,128)(2,1)} %collective-permute-done.1), channel_id=1, source_target_pairs={{0,1},{1,2},{2,3},{3,4},{4,5},{5,6},{6,7},{7,8},{8,9},{9,10},{10,1... | collective-permute-start | bytes 491528 | tf_op jit(solution)/shard_map/ppermute | solution.py:119
  31.5 11.8 %collective-permute-start.3 = (bf16[64,1,1280]{2,0,1:T(8,128)(2,1)}, bf16[64,1,1280]{2,0,1:T(8,128)(2,1)}, u32[]{:S(2)}, u32[]{:S(2)}) collective-permute-start(bf16[64,1,1280]{2,0,1:T(8,128)(2,1)} %collective-permute-done.2), channel_id=1, source_target_pairs={{0,1},{1,2},{2,3},{3,4},{4,5},{5,6},{6,7},{7,8},{8,9},{9,10},{10,1... | collective-permute-start | bytes 491528 | tf_op jit(solution)/shard_map/ppermute | solution.py:119
  43.3 7.7 %collective-permute-start.4 = (bf16[64,1,1280]{2,0,1:T(8,128)(2,1)}, bf16[64,1,1280]{2,0,1:T(8,128)(2,1)S(1)}, u32[]{:S(2)}, u32[]{:S(2)}) collective-permute-start(bf16[64,1,1280]{2,0,1:T(8,128)(2,1)} %collective-permute-done.3), channel_id=1, source_target_pairs={{0,1},{1,2},{2,3},{3,4},{4,5},{5,6},{6,7},{7,8},{8,9},{9,10},{10,1... | collective-permute-start | bytes 491528 | tf_op jit(solution)/shard_map/ppermute | solution.py:119
  51.0 78.0 %copy-start.6 = (bf16[64,1,1280]{2,0,1:T(8,128)(2,1)}, bf16[64,1,1280]{2,0,1:T(8,128)(2,1)S(1)}, u32[]{:S(2)}) copy-start(bf16[64,1,1280]{2,0,1:T(8,128)(2,1)S(1)} %collective-permute-done.4) | copy-start | bytes 491524
  51.0 9.9 %collective-permute-start.5 = (bf16[64,1,1280]{2,0,1:T(8,128)(2,1)S(1)}, bf16[64,1,1280]{2,0,1:T(8,128)(2,1)S(1)}, u32[]{:S(2)}, u32[]{:S(2)}) collective-permute-start(bf16[64,1,1280]{2,0,1:T(8,128)(2,1)S(1)} %collective-permute-done.4), channel_id=1, source_target_pairs={{0,1},{1,2},{2,3},{3,4},{4,5},{5,6},{6,7},{7,8},{8,9},{9,10},{10,1... | collective-permute-start | bytes 491528 | tf_op jit(solution)/shard_map/ppermute | solution.py:119
  51.0 70.3 %copy-start.27 = (f32[640]{0:T(1024)}, f32[640]{0:T(1024)S(1)}, u32[]{:S(2)}) copy-start(f32[640]{0:T(1024)S(1)} %broadcast_multiply_fusion.1) | copy-start | bytes 7684
  61.0 68.0 %copy-start.8 = (bf16[64,1,1280]{2,0,1:T(8,128)(2,1)}, bf16[64,1,1280]{2,0,1:T(8,128)(2,1)S(1)}, u32[]{:S(2)}) copy-start(bf16[64,1,1280]{2,0,1:T(8,128)(2,1)S(1)} %collective-permute-done.5) | copy-start | bytes 491524
  61.0 12.5 %collective-permute-start.6 = (bf16[64,1,1280]{2,0,1:T(8,128)(2,1)S(1)}, bf16[64,1,1280]{2,0,1:T(8,128)(2,1)S(1)}, u32[]{:S(2)}, u32[]{:S(2)}) collective-permute-start(bf16[64,1,1280]{2,0,1:T(8,128)(2,1)S(1)} %collective-permute-done.5), channel_id=1, source_target_pairs={{0,1},{1,2},{2,3},{3,4},{4,5},{5,6},{6,7},{7,8},{8,9},{9,10},{10,1... | collective-permute-start | bytes 491528 | tf_op jit(solution)/shard_map/ppermute | solution.py:119
  73.4 55.5 %copy-start.10 = (bf16[64,1,1280]{2,0,1:T(8,128)(2,1)}, bf16[64,1,1280]{2,0,1:T(8,128)(2,1)S(1)}, u32[]{:S(2)}) copy-start(bf16[64,1,1280]{2,0,1:T(8,128)(2,1)S(1)} %collective-permute-done.6) | copy-start | bytes 491524
  73.4 12.9 %collective-permute-start.7 = (bf16[64,1,1280]{2,0,1:T(8,128)(2,1)S(1)}, bf16[64,1,1280]{2,0,1:T(8,128)(2,1)S(1)}, u32[]{:S(2)}, u32[]{:S(2)}) collective-permute-start(bf16[64,1,1280]{2,0,1:T(8,128)(2,1)S(1)} %collective-permute-done.6), channel_id=1, source_target_pairs={{0,1},{1,2},{2,3},{3,4},{4,5},{5,6},{6,7},{7,8},{8,9},{9,10},{10,1... | collective-permute-start | bytes 491528 | tf_op jit(solution)/shard_map/ppermute | solution.py:119
  86.3 42.7 %copy-start.12 = (bf16[64,1,1280]{2,0,1:T(8,128)(2,1)}, bf16[64,1,1280]{2,0,1:T(8,128)(2,1)S(1)}, u32[]{:S(2)}) copy-start(bf16[64,1,1280]{2,0,1:T(8,128)(2,1)S(1)} %collective-permute-done.7) | copy-start | bytes 491524
  86.3 12.6 %collective-permute-start.8 = (bf16[64,1,1280]{2,0,1:T(8,128)(2,1)S(1)}, bf16[64,1,1280]{2,0,1:T(8,128)(2,1)S(1)}, u32[]{:S(2)}, u32[]{:S(2)}) collective-permute-start(bf16[64,1,1280]{2,0,1:T(8,128)(2,1)S(1)} %collective-permute-done.7), channel_id=1, source_target_pairs={{0,1},{1,2},{2,3},{3,4},{4,5},{5,6},{6,7},{7,8},{8,9},{9,10},{10,1... | collective-permute-start | bytes 491528 | tf_op jit(solution)/shard_map/ppermute | solution.py:119
  98.9 7.5 %collective-permute-start.9 = (bf16[64,1,1280]{2,0,1:T(8,128)(2,1)S(1)}, bf16[64,1,1280]{2,0,1:T(8,128)(2,1)S(1)}, u32[]{:S(2)}, u32[]{:S(2)}) collective-permute-start(bf16[64,1,1280]{2,0,1:T(8,128)(2,1)S(1)} %collective-permute-done.8), channel_id=1, source_target_pairs={{0,1},{1,2},{2,3},{3,4},{4,5},{5,6},{6,7},{7,8},{8,9},{9,10},{10,1... | collective-permute-start | bytes 491528 | tf_op jit(solution)/shard_map/ppermute | solution.py:119
  106.4 7.5 %collective-permute-start.10 = (bf16[64,1,1280]{2,0,1:T(8,128)(2,1)S(1)}, bf16[64,1,1280]{2,0,1:T(8,128)(2,1)S(1)}, u32[]{:S(2)}, u32[]{:S(2)}) collective-permute-start(bf16[64,1,1280]{2,0,1:T(8,128)(2,1)S(1)} %collective-permute-done.9), channel_id=1, source_target_pairs={{0,1},{1,2},{2,3},{3,4},{4,5},{5,6},{6,7},{7,8},{8,9},{9,10},{10,1... | collective-permute-start | bytes 491528 | tf_op jit(solution)/shard_map/ppermute | solution.py:119
  113.9 7.5 %collective-permute-start.11 = (bf16[64,1,1280]{2,0,1:T(8,128)(2,1)S(1)}, bf16[64,1,1280]{2,0,1:T(8,128)(2,1)S(1)}, u32[]{:S(2)}, u32[]{:S(2)}) collective-permute-start(bf16[64,1,1280]{2,0,1:T(8,128)(2,1)S(1)} %collective-permute-done.10), channel_id=1, source_target_pairs={{0,1},{1,2},{2,3},{3,4},{4,5},{5,6},{6,7},{7,8},{8,9},{9,10},{10,1... | collective-permute-start | bytes 491528 | tf_op jit(solution)/shard_map/ppermute | solution.py:119
  121.4 7.6 %collective-permute-start.12 = (bf16[64,1,1280]{2,0,1:T(8,128)(2,1)S(1)}, bf16[64,1,1280]{2,0,1:T(8,128)(2,1)}, u32[]{:S(2)}, u32[]{:S(2)}) collective-permute-start(bf16[64,1,1280]{2,0,1:T(8,128)(2,1)S(1)} %collective-permute-done.11), channel_id=1, source_target_pairs={{0,1},{1,2},{2,3},{3,4},{4,5},{5,6},{6,7},{7,8},{8,9},{9,10},{10,1... | collective-permute-start | bytes 491528 | tf_op jit(solution)/shard_map/ppermute | solution.py:119
  129.0 16.6 %collective-permute-start.13 = (bf16[64,1,1280]{2,0,1:T(8,128)(2,1)}, bf16[64,1,1280]{2,0,1:T(8,128)(2,1)}, u32[]{:S(2)}, u32[]{:S(2)}) collective-permute-start(bf16[64,1,1280]{2,0,1:T(8,128)(2,1)} %collective-permute-done.12), channel_id=1, source_target_pairs={{0,1},{1,2},{2,3},{3,4},{4,5},{5,6},{6,7},{7,8},{8,9},{9,10},{10,1... | collective-permute-start | bytes 491528 | tf_op jit(solution)/shard_map/ppermute | solution.py:119
  144.0 34.6 %copy-start.3 = (bf16[64,1,1280]{2,0,1:T(8,128)(2,1)S(1)}, bf16[64,1,1280]{2,0,1:T(8,128)(2,1)}, u32[]{:S(2)}) copy-start(bf16[64,1,1280]{2,0,1:T(8,128)(2,1)} %param.16) | copy-start | bytes 491524
  145.5 9.1 %collective-permute-start.14 = (bf16[64,1,1280]{2,0,1:T(8,128)(2,1)}, bf16[64,1,1280]{2,0,1:T(8,128)(2,1)}, u32[]{:S(2)}, u32[]{:S(2)}) collective-permute-start(bf16[64,1,1280]{2,0,1:T(8,128)(2,1)} %collective-permute-done.13), channel_id=1, source_target_pairs={{0,1},{1,2},{2,3},{3,4},{4,5},{5,6},{6,7},{7,8},{8,9},{9,10},{10,1... | collective-permute-start | bytes 491528 | tf_op jit(solution)/shard_map/ppermute | solution.py:119
  153.6 34.6 %copy-start.9 = (bf16[64,1,1280]{2,0,1:T(8,128)(2,1)S(1)}, bf16[64,1,1280]{2,0,1:T(8,128)(2,1)}, u32[]{:S(2)}) copy-start(bf16[64,1,1280]{2,0,1:T(8,128)(2,1)} %copy-done.8) | copy-start | bytes 491524
  153.6 35.3 %copy-start.7 = (bf16[64,1,1280]{2,0,1:T(8,128)(2,1)S(1)}, bf16[64,1,1280]{2,0,1:T(8,128)(2,1)}, u32[]{:S(2)}) copy-start(bf16[64,1,1280]{2,0,1:T(8,128)(2,1)} %copy-done.6) | copy-start | bytes 491524
  153.6 40.7 %copy-start.5 = (bf16[64,1,1280]{2,0,1:T(8,128)(2,1)S(1)}, bf16[64,1,1280]{2,0,1:T(8,128)(2,1)}, u32[]{:S(2)}) copy-start(bf16[64,1,1280]{2,0,1:T(8,128)(2,1)} %copy-done.4) | copy-start | bytes 491524
  154.6 41.0 %copy-start.28 = (f32[640]{0:T(1024)S(1)}, f32[640]{0:T(1024)}, u32[]{:S(2)}) copy-start(f32[640]{0:T(1024)} %copy-done.27) | copy-start | bytes 7684
  154.6 41.0 %copy-start.30 = (f32[640]{0:T(1024)S(1)}, f32[640]{0:T(1024)}, u32[]{:S(2)}) copy-start(f32[640]{0:T(1024)} %add_rsqrt_fusion) | copy-start | bytes 7684
  154.6 41.0 %copy-start.33 = (f32[1280]{0:T(1024)S(1)}, f32[1280]{0:T(1024)}, u32[]{:S(2)}) copy-start(f32[1280]{0:T(1024)} %param.14) | copy-start | bytes 15364
  248.1 15.3 %all-to-all-start = ((f32[1,64,1280]{2,0,1:T(1,128)}), f32[1,64,1280]{2,0,1:T(1,128)}, u32[]{:S(2)}, u32[]{:S(2)}) async-start(f32[1,64,1280]{2,0,1:T(1,128)} %copy.45), calls=%async_computation | async-start | bytes 655360 | tf_op jit(solution)/shard_map/all_to_all | solution.py:132
  (21 other events, 370.7 us)
Sparse Core Ops, SparseCore 0:
  9.8 92.8 all-gather.2
